TPU v7x, 512 devices: a whole 4x4x16 slice. The times are simulated.
512 devices in a mesh: island: 16 (over z), fsdp: 32 (over x, y, core).
Axes of the slice: x: 4, y: 4, z: 16, core: 2. Of those that a mesh axis runs over, the one named last changes fastest.
Arguments:
- activations: bfloat16 [16, 11776, 4096], P('island', 'fsdp'), may hold values from -6 to 6
- key_grad: bfloat16 [16, 11776, 512], P('island', 'fsdp'), may hold values from -0.0546875 to 0.0546875
- island_weight: float32 [16, 4096, 512], P('island', 'fsdp'), may hold values from -0.09375 to 0.09375
- adam_m: float32 [16, 4096, 512], P('island', 'fsdp'), may hold values from -6 to 6
- adam_v: float32 [16, 4096, 512], P('island', 'fsdp'), may hold values from 0.2 to 2
- anchor: float32 [16, 256, 512], P('island', 'fsdp'), may hold values from -0.09375 to 0.09375
- outer_momentum: float32 [16, 256, 512], P('island', 'fsdp'), may hold values from -0.09375 to 0.09375
Outputs:
- adam_m_next: float32 [16, 4096, 512], P('island', 'fsdp')
- adam_v_next: float32 [16, 4096, 512], P('island', 'fsdp')
- island_weight_next: float32 [4096, 512], P('fsdp')
- anchor_next: float32 [16, 256, 512], P('island', 'fsdp')
- momentum_next: float32 [16, 256, 512], P('island', 'fsdp')
All inputs are finite; a program needn't handle non-finite values.
Results may differ from a plain program's by a relative error of at most 0.0003.
Values may be sent and summed in bfloat16 or wider, within the bound.
A program may use at most 64 MiB of HBM per device.

v0:
```python
import jax
import jax.numpy as jnp
from jax import lax
from jax.sharding import PartitionSpec as P

beta_first = 0.9
beta_second = 0.95
epsilon = 1e-08
inner_rate = 0.0004
decay_rate = 0.1
outer_beta = 0.9
outer_rate = 0.7


def swapped(value, axis, bit):
    return lax.ppermute(value, axis, [(i, i ^ 1 << bit) for i in range(lax.axis_size(axis))])


def shards(activations, key_grad, island_weight, adam_m, adam_v, anchor, outer_momentum):
    inputs = activations[0]
    tangent = key_grad[0]
    row_count = island_weight.shape[1]
    columns = lax.all_to_all(inputs, "fsdp", split_axis=1, concat_axis=0, tiled=True)
    grad = lax.dot_general(
        columns,
        lax.all_gather(tangent, "fsdp", axis=0, tiled=True),
        (((0,), (0,)), ((), ())),
        preferred_element_type=jnp.float32,
    )
    m_next = beta_first * adam_m[0] + (1.0 - beta_first) * grad
    v_next = beta_second * adam_v[0] + (1.0 - beta_second) * grad * grad
    weight = island_weight[0]
    stepped = weight - inner_rate * (m_next / (jnp.sqrt(v_next) + epsilon) + decay_rate * weight)
    islands = lax.axis_size("island")
    levels = islands.bit_length() - 1
    share_rows = row_count // islands
    position = lax.axis_index("island")
    summed = stepped
    for bit in range(levels):
        summed = summed + swapped(summed, "island", bit)
    own_sum = lax.dynamic_slice_in_dim(summed, position * share_rows, share_rows, 0)
    anchor_block = anchor[0]
    shift = anchor_block - own_sum / float(islands)
    moment = outer_beta * outer_momentum[0] + shift
    new_anchor = anchor_block - outer_rate * (shift + outer_beta * moment)
    refreshed = lax.all_gather(new_anchor, "island", axis=0, tiled=True)
    return (m_next[None], v_next[None], refreshed, new_anchor[None], moment[None])


def solution(mesh):
    return jax.shard_map(
        shards,
        mesh=mesh,
        in_specs=(
            P("island", "fsdp", None),
            P("island", "fsdp", None),
            P("island", "fsdp", None),
            P("island", "fsdp", None),
            P("island", "fsdp", None),
            P("island", "fsdp", None),
            P("island", "fsdp", None),
        ),
        out_specs=(
            P("island", "fsdp", None),
            P("island", "fsdp", None),
            P("fsdp", None),
            P("island", "fsdp", None),
            P("island", "fsdp", None),
        ),
        check_vma=False,
    )
```

profile of v0, /device:TPU:2, one launch (start us, length us, event | category | flops | bytes accessed | tf_op | source)
XLA Modules:
  0.0 242.4 jit_solution(13812907711596420552)
XLA Ops:
  7.2 0.0 all-gather.3.cloned.1.call-start
  7.2 0.7 all-gather.3.cloned.1.call-update
  7.9 2.6 %copy.14 = bf16[46,8,32,128]{3,2,1,0:T(8,128)(2,1)S(1)} copy(bf16[46,8,32,128]{3,1,2,0:T(8,128)(2,1)} %bitcast.55) | data formatting | bytes 6029312
  10.5 1.2 copy.13
  11.7 0.0 copy-start
  11.7 0.0 copy-start.1
  11.7 50.5 %all_to_all.19 = bf16[368,32,128]{2,0,1:T(8,128)(2,1)S(1)} all-to-all(bf16[368,32,128]{2,0,1:T(8,128)(2,1)S(1)} %copy.13), channel_id=1, replica_groups=mesh['island'=16,'fsdp'=32] {'fsdp'}, dimensions={1} | all-to-all | bytes 6029312 | tf_op jit(solution)/shard_map/all_to_all | solution.py:23
  62.3 47.1 %all-gather.3.cloned.1.call-done = bf16[1,11776,512]{2,1,0:T(8,128)(2,1)} async-done(((bf16[1,368,512]{2,1,0:T(8,128)(2,1)}), bf16[1,11776,512]{2,1,0:T(8,128)(2,1)}) %all-gather.3.cloned.1.call-update) | async-done | bytes 12058640 | tf_op jit(solution)/shard_map/all_gather | solution.py:26
  109.4 0.0 copy-done
  109.4 0.0 copy-done.1
  109.4 7.1 %bitcast_subtract_fusion = (f32[128,512]{1,0:T(8,128)S(1)}, f32[1,128,512]{2,1,0:T(8,128)}, f32[1,128,512]{2,1,0:T(8,128)}) fusion(f32[1,128,512]{2,1,0:T(8,128)S(1)} %copy-done, f32[1,128,512]{2,1,0:T(8,128)S(1)} %copy-done.1, f32[1,128,512]{2,1,0:T(8,128)} %param.11, bf16[11776,128]{1,0:T(8,128)(2,1)S(1)} %bitcast.53, ...), kind=kOutput, calls=%fused_computation.4 | convolution fusion | flops 1544355840 | bytes 16646144 | tf_op jit(solution)/shard_map/dot_general | solution.py:24
  116.5 3.4 %collective-permute-start = (f32[128,512]{1,0:T(8,128)S(1)}, f32[128,512]{1,0:T(8,128)S(1)}, u32[]{:S(2)}, u32[]{:S(2)}) collective-permute-start(f32[128,512]{1,0:T(8,128)S(1)} %get-tuple-element.7), channel_id=1, source_target_pairs={{0,32},{32,0},{64,96},{96,64},{128,160},{160,128},{192,224},{224,1... | collective-permute-start | bytes 786440 | tf_op jit(solution)/shard_map/ppermute | solution.py:16
  120.0 6.9 %collective-permute-done = f32[128,512]{1,0:T(8,128)S(1)} collective-permute-done((f32[128,512]{1,0:T(8,128)S(1)}, f32[128,512]{1,0:T(8,128)S(1)}, u32[]{:S(2)}, u32[]{:S(2)}) %collective-permute-start) | collective-permute-done | bytes 262176 | tf_op jit(solution)/shard_map/ppermute | solution.py:16
  126.9 4.5 %collective-permute-start.1 = (f32[128,512]{1,0:T(8,128)S(1)}, f32[128,512]{1,0:T(8,128)S(1)}, u32[]{:S(2)}, u32[]{:S(2)}) collective-permute-start(f32[128,512]{1,0:T(8,128)S(1)} %add.41), channel_id=1, source_target_pairs={{0,64},{32,96},{64,0},{96,32},{128,192},{160,224},{192,128},{224,1... | collective-permute-start | bytes 786440 | tf_op jit(solution)/shard_map/ppermute | solution.py:16
  131.4 11.6 %collective-permute-done.1 = f32[128,512]{1,0:T(8,128)S(1)} collective-permute-done((f32[128,512]{1,0:T(8,128)S(1)}, f32[128,512]{1,0:T(8,128)S(1)}, u32[]{:S(2)}, u32[]{:S(2)}) %collective-permute-start.1) | collective-permute-done | bytes 262176 | tf_op jit(solution)/shard_map/ppermute | solution.py:16
  143.0 7.6 %collective-permute-start.2 = (f32[128,512]{1,0:T(8,128)S(1)}, f32[128,512]{1,0:T(8,128)S(1)}, u32[]{:S(2)}, u32[]{:S(2)}) collective-permute-start(f32[128,512]{1,0:T(8,128)S(1)} %add.42), channel_id=1, source_target_pairs={{0,128},{32,160},{64,192},{96,224},{128,0},{160,32},{192,64},{224,... | collective-permute-start | bytes 786440 | tf_op jit(solution)/shard_map/ppermute | solution.py:16
  150.7 21.2 %collective-permute-done.2 = f32[128,512]{1,0:T(8,128)S(1)} collective-permute-done((f32[128,512]{1,0:T(8,128)S(1)}, f32[128,512]{1,0:T(8,128)S(1)}, u32[]{:S(2)}, u32[]{:S(2)}) %collective-permute-start.2) | collective-permute-done | bytes 262176 | tf_op jit(solution)/shard_map/ppermute | solution.py:16
  171.9 11.5 %collective-permute-start.3 = (f32[128,512]{1,0:T(8,128)S(1)}, f32[128,512]{1,0:T(8,128)S(1)}, u32[]{:S(2)}, u32[]{:S(2)}) collective-permute-start(f32[128,512]{1,0:T(8,128)S(1)} %add.43), channel_id=1, source_target_pairs={{0,256},{32,288},{64,320},{96,352},{128,384},{160,416},{192,448},{... | collective-permute-start | bytes 786440 | tf_op jit(solution)/shard_map/ppermute | solution.py:16
  183.4 22.2 %collective-permute-done.3 = f32[128,512]{1,0:T(8,128)S(1)} collective-permute-done((f32[128,512]{1,0:T(8,128)S(1)}, f32[128,512]{1,0:T(8,128)S(1)}, u32[]{:S(2)}, u32[]{:S(2)}) %collective-permute-start.3) | collective-permute-done | bytes 262176 | tf_op jit(solution)/shard_map/ppermute | solution.py:16
  205.6 0.0 copy-done.3
  205.6 1.3 fusion.9
  207.0 27.9 %all_gather.7 = f32[128,512]{1,0:T(8,128)S(1)} all-gather(f32[8,512]{1,0:T(8,128)S(1)} %get-tuple-element.6), channel_id=1, replica_groups=mesh['island'=16,'fsdp'=32] {'island'}, dimensions={0}, use_global_device_ids=true | all-gather | bytes 278528 | tf_op jit(solution)/shard_map/all_gather | solution.py:46
  234.9 0.7 copy.16
  235.6 0.0 copy-done.2
  (5 shorter events, 0.1 us)
Async XLA Ops:
  7.2 102.2 %all-gather.3.cloned.1.call-start = ((), (), s32[]{:S(2)}) async-start(), calls=%async_computation.1 | async-start | bytes 12435456 | tf_op jit(solution)/shard_map/all_gather | solution.py:26
  11.7 97.6 %copy-start = (f32[1,128,512]{2,1,0:T(8,128)S(1)}, f32[1,128,512]{2,1,0:T(8,128)}, u32[]{:S(2)}) copy-start(f32[1,128,512]{2,1,0:T(8,128)} %param.9) | copy-start | bytes 786436
  11.7 97.6 %copy-start.1 = (f32[1,128,512]{2,1,0:T(8,128)S(1)}, f32[1,128,512]{2,1,0:T(8,128)}, u32[]{:S(2)}) copy-start(f32[1,128,512]{2,1,0:T(8,128)} %param.10) | copy-start | bytes 786436
  109.4 96.3 %copy-start.3 = (f32[1,8,512]{2,1,0:T(8,128)S(1)}, f32[1,8,512]{2,1,0:T(8,128)}, u32[]{:S(2)}) copy-start(f32[1,8,512]{2,1,0:T(8,128)} %param.13) | copy-start | bytes 49156
  116.5 10.3 %collective-permute-start = (f32[128,512]{1,0:T(8,128)S(1)}, f32[128,512]{1,0:T(8,128)S(1)}, u32[]{:S(2)}, u32[]{:S(2)}) collective-permute-start(f32[128,512]{1,0:T(8,128)S(1)} %get-tuple-element.7), channel_id=1, source_target_pairs={{0,32},{32,0},{64,96},{96,64},{128,160},{160,128},{192,224},{224,1... | collective-permute-start | bytes 786440 | tf_op jit(solution)/shard_map/ppermute | solution.py:16
  126.9 16.1 %collective-permute-start.1 = (f32[128,512]{1,0:T(8,128)S(1)}, f32[128,512]{1,0:T(8,128)S(1)}, u32[]{:S(2)}, u32[]{:S(2)}) collective-permute-start(f32[128,512]{1,0:T(8,128)S(1)} %add.41), channel_id=1, source_target_pairs={{0,64},{32,96},{64,0},{96,32},{128,192},{160,224},{192,128},{224,1... | collective-permute-start | bytes 786440 | tf_op jit(solution)/shard_map/ppermute | solution.py:16
  143.0 28.9 %collective-permute-start.2 = (f32[128,512]{1,0:T(8,128)S(1)}, f32[128,512]{1,0:T(8,128)S(1)}, u32[]{:S(2)}, u32[]{:S(2)}) collective-permute-start(f32[128,512]{1,0:T(8,128)S(1)} %add.42), channel_id=1, source_target_pairs={{0,128},{32,160},{64,192},{96,224},{128,0},{160,32},{192,64},{224,... | collective-permute-start | bytes 786440 | tf_op jit(solution)/shard_map/ppermute | solution.py:16
  171.9 33.7 %collective-permute-start.3 = (f32[128,512]{1,0:T(8,128)S(1)}, f32[128,512]{1,0:T(8,128)S(1)}, u32[]{:S(2)}, u32[]{:S(2)}) collective-permute-start(f32[128,512]{1,0:T(8,128)S(1)} %add.43), channel_id=1, source_target_pairs={{0,256},{32,288},{64,320},{96,352},{128,384},{160,416},{192,448},{... | collective-permute-start | bytes 786440 | tf_op jit(solution)/shard_map/ppermute | solution.py:16
  207.0 28.6 %copy-start.2 = (f32[8,512]{1,0:T(8,128)}, f32[8,512]{1,0:T(8,128)S(1)}, u32[]{:S(2)}) copy-start(f32[8,512]{1,0:T(8,128)S(1)} %get-tuple-element.6) | copy-start | bytes 49156
Sparse Core Ops, SparseCore 0:
  11.1 98.1 all-gather.2
where the time goes:
time: 243 us; the launch traced here: 242 us
  waiting for transfers between devices  110 us (45%)
  blocking collectives  78.4 us (32%)
  starting transfers between devices  27.1 us (11%)
  between operations  14.1 us (6%)
  matrix products  7.15 us (3%)
  local copies, waits for them, and re-layouts  4.52 us (2%)
    ppermute x4, waiting for transfers between devices, swapped(): lax.ppermute(value, axis, [(i, i ^ 1 << bit) for i in range(lax.axis_size...  61.9 us
    all_to_all x1, blocking collectives, shards(): lax.all_to_all(inputs, 'fsdp', split_axis=1, concat_axis=0, tiled=True)  50.5 us
    all_gather x1, waiting for transfers between devices, shards(): lax.all_gather(tangent, 'fsdp', axis=0, tiled=True)  47.1 us
    all_gather x1, blocking collectives, shards(): refreshed = lax.all_gather(new_anchor, 'island', axis=0, tiled=True)  27.9 us
    ppermute x4, starting transfers between devices, swapped(): lax.ppermute(value, axis, [(i, i ^ 1 << bit) for i in range(lax.axis_size...  27.1 us
    dot_general x1, matrix products, shards(): lax.dot_general(columns, lax.all_gather(tangent, 'fsdp', axis=0, tiled=Tr...  7.15 us
  transfers between devices with their start and end apart: 5, of which 5 were waited for; matrix products, arithmetic and copies ran while one was open for 2% of the time, Pallas kernels for 0%

commit v1 on v0

--- a/solution.py
+++ b/solution.py
@@ -10,6 +10,11 @@
 decay_rate = 0.1
 outer_beta = 0.9
 outer_rate = 0.7
+
+
+def gather_by_exchange(array, axis, dim):
+    copies = jnp.concatenate([array] * lax.axis_size(axis), axis=dim)
+    return lax.all_to_all(copies, axis, dim, dim, tiled=True)
 
 
 def swapped(value, axis, bit):
@@ -43,7 +48,7 @@
     shift = anchor_block - own_sum / float(islands)
     moment = outer_beta * outer_momentum[0] + shift
     new_anchor = anchor_block - outer_rate * (shift + outer_beta * moment)
-    refreshed = lax.all_gather(new_anchor, "island", axis=0, tiled=True)
+    refreshed = gather_by_exchange(new_anchor, "island", 0)
     return (m_next[None], v_next[None], refreshed, new_anchor[None], moment[None])
 
 

time: 243 us -> 238 us (0.979)
  blocking collectives: 78.4 us -> 73.5 us
    all_gather x1 -> x0, blocking collectives: 27.9 us -> none  [shards(): refreshed = lax.all_gather(new_anchor, 'island', axis=0, tiled=True)]
    all_to_all x0 -> x1, blocking collectives: none -> 22.9 us  [gather_by_exchange(): return lax.all_to_all(copies, axis, dim, dim, tiled=True)]
where the time goes in v1:
time: 238 us; the launch traced here: 237 us
  waiting for transfers between devices  109 us (46%)
  blocking collectives  73.5 us (31%)
  starting transfers between devices  27.1 us (11%)
  between operations  14.2 us (6%)
  matrix products  7.15 us (3%)
  local copies, waits for them, and re-layouts  4.57 us (2%)
    ppermute x4, waiting for transfers between devices, swapped(): lax.ppermute(value, axis, [(i, i ^ 1 << bit) for i in range(lax.axis_size...  61.6 us
    all_to_all x1, blocking collectives, shards(): lax.all_to_all(inputs, 'fsdp', split_axis=1, concat_axis=0, tiled=True)  50.5 us
    all_gather x1, waiting for transfers between devices, shards(): lax.all_gather(tangent, 'fsdp', axis=0, tiled=True)  47.1 us
    ppermute x4, starting transfers between devices, swapped(): lax.ppermute(value, axis, [(i, i ^ 1 << bit) for i in range(lax.axis_size...  27.1 us
    all_to_all x1, blocking collectives, gather_by_exchange(): return lax.all_to_all(copies, axis, dim, dim, tiled=True)  22.9 us
    dot_general x1, matrix products, shards(): lax.dot_general(columns, lax.all_gather(tangent, 'fsdp', axis=0, tiled=Tr...  7.15 us
  transfers between devices with their start and end apart: 5, of which 5 were waited for; matrix products, arithmetic and copies ran while one was open for 2% of the time, Pallas kernels for 0%

profile of v1, /device:TPU:2, one launch (start us, length us, event | category | flops | bytes accessed | tf_op | source)
XLA Modules:
  0.0 237.4 jit_solution(18385744522132543502)
XLA Ops:
  7.2 0.0 all-gather.3.cloned.1.call-start
  7.2 0.7 all-gather.3.cloned.1.call-update
  7.9 2.6 %copy.14 = bf16[46,8,32,128]{3,2,1,0:T(8,128)(2,1)S(1)} copy(bf16[46,8,32,128]{3,1,2,0:T(8,128)(2,1)} %bitcast.60) | data formatting | bytes 6029312
  10.5 1.2 copy.13
  11.7 0.0 copy-start.1
  11.7 0.0 copy-start.2
  11.7 50.5 %all_to_all.31 = bf16[368,32,128]{2,0,1:T(8,128)(2,1)S(1)} all-to-all(bf16[368,32,128]{2,0,1:T(8,128)(2,1)S(1)} %copy.13), channel_id=1, replica_groups=mesh['island'=16,'fsdp'=32] {'fsdp'}, dimensions={1} | all-to-all | bytes 6029312 | tf_op jit(solution)/shard_map/all_to_all | solution.py:28
  62.3 47.1 %all-gather.3.cloned.1.call-done = bf16[1,11776,512]{2,1,0:T(8,128)(2,1)} async-done(((bf16[1,368,512]{2,1,0:T(8,128)(2,1)}), bf16[1,11776,512]{2,1,0:T(8,128)(2,1)}) %all-gather.3.cloned.1.call-update) | async-done | bytes 12058640 | tf_op jit(solution)/shard_map/all_gather | solution.py:31
  109.4 0.0 copy-done.1
  109.4 0.0 copy-done.2
  109.4 7.1 %bitcast_subtract_fusion = (f32[128,512]{1,0:T(8,128)S(1)}, f32[1,128,512]{2,1,0:T(8,128)}, f32[1,128,512]{2,1,0:T(8,128)}) fusion(f32[1,128,512]{2,1,0:T(8,128)S(1)} %copy-done.1, f32[1,128,512]{2,1,0:T(8,128)S(1)} %copy-done.2, f32[1,128,512]{2,1,0:T(8,128)} %param.11, bf16[11776,128]{1,0:T(8,128)(2,1)S(1)} %bitcast.57, ...), kind=kOutput, calls=%fused_computation.4 | convolution fusion | flops 1544355840 | bytes 16646144 | tf_op jit(solution)/shard_map/dot_general | solution.py:29
  116.5 3.4 %collective-permute-start = (f32[128,512]{1,0:T(8,128)S(1)}, f32[128,512]{1,0:T(8,128)S(1)}, u32[]{:S(2)}, u32[]{:S(2)}) collective-permute-start(f32[128,512]{1,0:T(8,128)S(1)} %get-tuple-element.8), channel_id=1, source_target_pairs={{0,32},{32,0},{64,96},{96,64},{128,160},{160,128},{192,224},{224,1... | collective-permute-start | bytes 786440 | tf_op jit(solution)/shard_map/ppermute | solution.py:21
  120.0 6.9 %collective-permute-done = f32[128,512]{1,0:T(8,128)S(1)} collective-permute-done((f32[128,512]{1,0:T(8,128)S(1)}, f32[128,512]{1,0:T(8,128)S(1)}, u32[]{:S(2)}, u32[]{:S(2)}) %collective-permute-start) | collective-permute-done | bytes 262176 | tf_op jit(solution)/shard_map/ppermute | solution.py:21
  126.9 4.5 %collective-permute-start.1 = (f32[128,512]{1,0:T(8,128)S(1)}, f32[128,512]{1,0:T(8,128)S(1)}, u32[]{:S(2)}, u32[]{:S(2)}) collective-permute-start(f32[128,512]{1,0:T(8,128)S(1)} %add.41), channel_id=1, source_target_pairs={{0,64},{32,96},{64,0},{96,32},{128,192},{160,224},{192,128},{224,1... | collective-permute-start | bytes 786440 | tf_op jit(solution)/shard_map/ppermute | solution.py:21
  131.4 11.6 %collective-permute-done.1 = f32[128,512]{1,0:T(8,128)S(1)} collective-permute-done((f32[128,512]{1,0:T(8,128)S(1)}, f32[128,512]{1,0:T(8,128)S(1)}, u32[]{:S(2)}, u32[]{:S(2)}) %collective-permute-start.1) | collective-permute-done | bytes 262176 | tf_op jit(solution)/shard_map/ppermute | solution.py:21
  143.0 7.6 %collective-permute-start.2 = (f32[128,512]{1,0:T(8,128)S(1)}, f32[128,512]{1,0:T(8,128)S(1)}, u32[]{:S(2)}, u32[]{:S(2)}) collective-permute-start(f32[128,512]{1,0:T(8,128)S(1)} %add.42), channel_id=1, source_target_pairs={{0,128},{32,160},{64,192},{96,224},{128,0},{160,32},{192,64},{224,... | collective-permute-start | bytes 786440 | tf_op jit(solution)/shard_map/ppermute | solution.py:21
  150.7 21.2 %collective-permute-done.2 = f32[128,512]{1,0:T(8,128)S(1)} collective-permute-done((f32[128,512]{1,0:T(8,128)S(1)}, f32[128,512]{1,0:T(8,128)S(1)}, u32[]{:S(2)}, u32[]{:S(2)}) %collective-permute-start.2) | collective-permute-done | bytes 262176 | tf_op jit(solution)/shard_map/ppermute | solution.py:21
  171.9 11.5 %collective-permute-start.3 = (f32[128,512]{1,0:T(8,128)S(1)}, f32[128,512]{1,0:T(8,128)S(1)}, u32[]{:S(2)}, u32[]{:S(2)}) collective-permute-start(f32[128,512]{1,0:T(8,128)S(1)} %add.43), channel_id=1, source_target_pairs={{0,256},{32,288},{64,320},{96,352},{128,384},{160,416},{192,448},{... | collective-permute-start | bytes 786440 | tf_op jit(solution)/shard_map/ppermute | solution.py:21
  183.4 21.9 %collective-permute-done.3 = f32[128,512]{1,0:T(8,128)S(1)} collective-permute-done((f32[128,512]{1,0:T(8,128)S(1)}, f32[128,512]{1,0:T(8,128)S(1)}, u32[]{:S(2)}, u32[]{:S(2)}) %collective-permute-start.3) | collective-permute-done | bytes 262176 | tf_op jit(solution)/shard_map/ppermute | solution.py:21
  205.4 0.0 copy-done.3
  205.4 1.3 constant_dynamic-update-slice_fusion.15
  206.9 22.9 %all_to_all.32 = f32[16,8,512]{2,1,0:T(8,128)S(1)} all-to-all(f32[16,8,512]{2,1,0:T(8,128)S(1)} %bitcast.62), channel_id=1, replica_groups=mesh['island'=16,'fsdp'=32] {'island'}, dimensions={0} | all-to-all | bytes 524288 | tf_op jit(solution)/shard_map/all_to_all | solution.py:17
  229.8 0.7 copy.31
  230.5 0.0 copy-done
  (20 shorter events, 0.2 us)
Async XLA Ops:
  7.2 102.2 %all-gather.3.cloned.1.call-start = ((), (), s32[]{:S(2)}) async-start(), calls=%async_computation.2 | async-start | bytes 12435456 | tf_op jit(solution)/shard_map/all_gather | solution.py:31
  11.7 97.6 %copy-start.1 = (f32[1,128,512]{2,1,0:T(8,128)S(1)}, f32[1,128,512]{2,1,0:T(8,128)}, u32[]{:S(2)}) copy-start(f32[1,128,512]{2,1,0:T(8,128)} %param.9) | copy-start | bytes 786436
  11.7 97.6 %copy-start.2 = (f32[1,128,512]{2,1,0:T(8,128)S(1)}, f32[1,128,512]{2,1,0:T(8,128)}, u32[]{:S(2)}) copy-start(f32[1,128,512]{2,1,0:T(8,128)} %param.10) | copy-start | bytes 786436
  109.4 96.0 %copy-start.3 = (f32[1,8,512]{2,1,0:T(8,128)S(1)}, f32[1,8,512]{2,1,0:T(8,128)}, u32[]{:S(2)}) copy-start(f32[1,8,512]{2,1,0:T(8,128)} %param.13) | copy-start | bytes 49156
  116.5 10.3 %collective-permute-start = (f32[128,512]{1,0:T(8,128)S(1)}, f32[128,512]{1,0:T(8,128)S(1)}, u32[]{:S(2)}, u32[]{:S(2)}) collective-permute-start(f32[128,512]{1,0:T(8,128)S(1)} %get-tuple-element.8), channel_id=1, source_target_pairs={{0,32},{32,0},{64,96},{96,64},{128,160},{160,128},{192,224},{224,1... | collective-permute-start | bytes 786440 | tf_op jit(solution)/shard_map/ppermute | solution.py:21
  126.9 16.1 %collective-permute-start.1 = (f32[128,512]{1,0:T(8,128)S(1)}, f32[128,512]{1,0:T(8,128)S(1)}, u32[]{:S(2)}, u32[]{:S(2)}) collective-permute-start(f32[128,512]{1,0:T(8,128)S(1)} %add.41), channel_id=1, source_target_pairs={{0,64},{32,96},{64,0},{96,32},{128,192},{160,224},{192,128},{224,1... | collective-permute-start | bytes 786440 | tf_op jit(solution)/shard_map/ppermute | solution.py:21
  143.0 28.9 %collective-permute-start.2 = (f32[128,512]{1,0:T(8,128)S(1)}, f32[128,512]{1,0:T(8,128)S(1)}, u32[]{:S(2)}, u32[]{:S(2)}) collective-permute-start(f32[128,512]{1,0:T(8,128)S(1)} %add.42), channel_id=1, source_target_pairs={{0,128},{32,160},{64,192},{96,224},{128,0},{160,32},{192,64},{224,... | collective-permute-start | bytes 786440 | tf_op jit(solution)/shard_map/ppermute | solution.py:21
  171.9 33.5 %collective-permute-start.3 = (f32[128,512]{1,0:T(8,128)S(1)}, f32[128,512]{1,0:T(8,128)S(1)}, u32[]{:S(2)}, u32[]{:S(2)}) collective-permute-start(f32[128,512]{1,0:T(8,128)S(1)} %add.43), channel_id=1, source_target_pairs={{0,256},{32,288},{64,320},{96,352},{128,384},{160,416},{192,448},{... | collective-permute-start | bytes 786440 | tf_op jit(solution)/shard_map/ppermute | solution.py:21
  206.7 23.8 %copy-start = (f32[8,512]{1,0:T(8,128)}, f32[8,512]{1,0:T(8,128)S(1)}, u32[]{:S(2)}) copy-start(f32[8,512]{1,0:T(8,128)S(1)} %get-tuple-element.6) | copy-start | bytes 49156
Sparse Core Ops, SparseCore 0:
  11.1 98.1 all-gather.2
